TPU v7x, 32 devices: a whole 2x2x4 slice. The times are simulated.
32 devices in a mesh: dp: 4 (over z), seq: 8 (over y, x, core).
Axes of the slice: x: 2, y: 2, z: 4, core: 2. Of those that a mesh axis runs over, the one named last changes fastest.
Arguments:
- signal: bfloat16 [8, 1024, 1536], P('dp', 'seq'), may hold values from -6 to 6
- dilated_tap_weight: bfloat16 [3, 1536, 768], P(None, 'dp'), may hold values from -0.09375 to 0.09375
- out_weight: bfloat16 [768, 1536], P(None, 'dp'), may hold values from -0.21875 to 0.21875
- cotangent: bfloat16 [8, 1024, 1536], P('dp', 'seq'), may hold values from -6 to 6
Outputs:
- result: bfloat16 [8, 1024, 1536], P('dp', 'seq')
- grad_signal: bfloat16 [8, 1024, 1536], P('dp', 'seq')
All inputs are finite; a program needn't handle non-finite values.
Results may differ from a plain program's by a relative error of at most 0.0034.
Values may be sent and summed in bfloat16 or wider, within the bound.
No kernel may reach another device: no remote copies, remote signals or barrier semaphores. Data moves between devices by JAX's collectives and lax.ppermute only.
A program may use at most 64 MiB of HBM per device.

v0:
```python
import jax
import jax.numpy as jnp
from jax import lax
from jax.sharding import PartitionSpec as P

DILATION_STEP = 32


def extended(block, sides, width):
    for axis, dim in sides:
        count = lax.axis_size(axis)
        forward = [(i, i + 1) for i in range(count - 1)]
        backward = [(target, source) for source, target in forward]
        low = lax.ppermute(
            lax.slice_in_dim(block, block.shape[dim] - width, None, axis=dim), axis, forward
        )
        high = lax.ppermute(lax.slice_in_dim(block, 0, width, axis=dim), axis, backward)
        block = jnp.concatenate([low, block, high], axis=dim)
    return block


def gelu_pull(point, grad):
    _, pull = jax.vjp(jax.nn.gelu, point)
    return pull(grad)[0]


def forward_taps(gelu_output, padded_signal, convolution_filter):
    sequence_length = gelu_output.shape[1]
    preactivation = jnp.einsum(
        "xzi,iv->xzv",
        padded_signal[:, 0:sequence_length],
        convolution_filter[0],
        preferred_element_type=jnp.float32,
    )
    preactivation = preactivation + jnp.einsum(
        "xzi,iv->xzv",
        padded_signal[:, DILATION_STEP : DILATION_STEP + sequence_length],
        convolution_filter[1],
        preferred_element_type=jnp.float32,
    )
    preactivation = preactivation + jnp.einsum(
        "xzi,iv->xzv",
        padded_signal[:, 2 * DILATION_STEP : 2 * DILATION_STEP + sequence_length],
        convolution_filter[2],
        preferred_element_type=jnp.float32,
    )
    return preactivation


def backward_taps(gradient_preactivation, gradient_padded_input, convolution_filter):
    sequence_length = gradient_preactivation.shape[1]
    gradient_activation = jnp.einsum(
        "wth,ch->wtc",
        gradient_padded_input[:, 2 * DILATION_STEP : 2 * DILATION_STEP + sequence_length],
        convolution_filter[0],
        preferred_element_type=jnp.float32,
    )
    gradient_activation = gradient_activation + jnp.einsum(
        "wth,ch->wtc",
        gradient_padded_input[:, DILATION_STEP : DILATION_STEP + sequence_length],
        convolution_filter[1],
        preferred_element_type=jnp.float32,
    )
    gradient_activation = gradient_activation + jnp.einsum(
        "wth,ch->wtc",
        gradient_padded_input[:, 0:sequence_length],
        convolution_filter[2],
        preferred_element_type=jnp.float32,
    )
    return gradient_activation


def per_device(signal, dilated_tap_weight, out_weight, cotangent):
    convolution_filter, output_map = (
        lax.all_gather(dilated_tap_weight, "dp", axis=1, tiled=True),
        lax.all_gather(out_weight, "dp", axis=1, tiled=True),
    )
    signal_wide = signal.astype(jnp.float32)
    gelu_output = jax.nn.gelu(signal_wide).astype(jnp.bfloat16)
    padded_signal = extended(gelu_output, (("seq", 1),), DILATION_STEP)
    preactivation = forward_taps(gelu_output, padded_signal, convolution_filter)
    active = jax.nn.gelu(preactivation).astype(jnp.bfloat16)
    output = signal_wide + jnp.einsum(
        "wth,hc->wtc", active, output_map, preferred_element_type=jnp.float32
    )
    grad_active = jnp.einsum(
        "wtc,hc->wth", cotangent, output_map, preferred_element_type=jnp.float32
    )
    gradient_preactivation = gelu_pull(preactivation, grad_active).astype(jnp.bfloat16)
    gradient_padded_input = extended(gradient_preactivation, (("seq", 1),), DILATION_STEP)
    gradient_activation = backward_taps(
        gradient_preactivation, gradient_padded_input, convolution_filter
    )
    grad_in = cotangent.astype(jnp.float32) + gelu_pull(signal_wide, gradient_activation)
    return (output.astype(jnp.bfloat16), grad_in.astype(jnp.bfloat16))


def solution(mesh):
    return jax.shard_map(
        per_device,
        mesh=mesh,
        in_specs=(P("dp", "seq", None), P(None, "dp", None), P(None, "dp"), P("dp", "seq", None)),
        out_specs=(P("dp", "seq", None), P("dp", "seq", None)),
        check_vma=False,
    )
```

profile of v0, /device:TPU:1, one launch (start us, length us, event | category | flops | bytes accessed | tf_op | source)
XLA Modules:
  0.0 213.3 jit_solution(15958082162178033405)
XLA Ops:
  7.2 0.0 copy-start
  7.2 0.0 all-gather.3.cloned.1.call-start
  7.2 0.7 all-gather.3.cloned.1.call-update
  7.9 0.0 all-gather.5.cloned.1.call-start
  8.0 0.7 all-gather.5.cloned.1.call-update
  8.7 0.0 copy-done
  8.7 0.5 fusion.18
  9.2 4.5 %collective-permute-start = (bf16[2,32,1536]{2,1,0:T(8,128)(2,1)S(1)}, bf16[2,32,1536]{2,1,0:T(8,128)(2,1)S(1)}, u32[]{:S(2)}, u32[]{:S(2)}) collective-permute-start(bf16[2,32,1536]{2,1,0:T(8,128)(2,1)S(1)} %get-tuple-element.2), channel_id=1, source_target_pairs={{0,1},{1,2},{2,3},{3,4},{4,5},{5,6},{6,7},{8,9},{9,10},{10,11},{11... | collective-permute-start | bytes 589832 | tf_op jit(solution)/shard_map/ppermute | solution.py:14
  13.8 1.9 collective-permute-start.1
  15.7 124.4 %all-gather.3.cloned.1.call-done = bf16[3,1536,768]{2,1,0:T(8,128)(2,1)} async-done(((bf16[3,384,768]{2,1,0:T(8,128)(2,1)}), bf16[3,1536,768]{2,1,0:T(8,128)(2,1)}) %all-gather.3.cloned.1.call-update) | async-done | bytes 7077904 | tf_op jit(solution)/shard_map/all_gather | solution.py:75
  140.1 2.9 %fusion.8 = f32[2,128,768]{2,1,0:T(8,128)S(1)} fusion(bf16[3,1536,768]{2,1,0:T(8,128)(2,1)} %all-gather.3.cloned.1.call-done, bf16[2,128,1536]{2,1,0:T(8,128)(2,1)S(1)} %copy-done), kind=kOutput, calls=%fused_computation.18 | convolution fusion | flops 607911936 | bytes 3932160 | tf_op jit(solution)/shard_map/xzi,iv->xzv/dot_general | solution.py:35
  143.0 0.0 collective-permute-done.1
  143.0 0.8 copy-done.1
  143.8 0.8 fusion.10
  144.6 0.0 copy-start.3
  144.6 0.0 collective-permute-done
  144.6 0.8 fusion.22
  145.4 44.6 %all-gather.5.cloned.1.call-done = bf16[768,1536]{1,0:T(8,128)(2,1)} async-done(((bf16[768,384]{1,0:T(8,128)(2,1)}), bf16[768,1536]{1,0:T(8,128)(2,1)}) %all-gather.5.cloned.1.call-update) | async-done | bytes 2359312 | tf_op jit(solution)/shard_map/all_gather | solution.py:76
  190.0 0.0 copy-done.3
  190.0 2.9 %fusion.29 = bf16[2,128,768]{2,1,0:T(8,128)(2,1)S(1)} fusion(f32[2,128,768]{2,1,0:T(8,128)S(1)} %fusion.22, bf16[2,128,1536]{2,1,0:T(8,128)(2,1)S(1)} %copy-done.3, bf16[768,1536]{1,0:T(8,128)(2,1)} %all-gather.5.cloned.1.call-done), kind=kOutput, calls=%fused_computation.41 | convolution fusion | flops 607911936 | bytes 4325376 | tf_op jit(solution)/shard_map/wtc,hc->wth/dot_general | solution.py:86
  192.9 2.6 %collective-permute-start.2 = (bf16[2,32,768]{2,1,0:T(8,128)(2,1)S(1)}, bf16[2,32,768]{2,1,0:T(8,128)(2,1)S(1)}, u32[]{:S(2)}, u32[]{:S(2)}) collective-permute-start(bf16[2,32,768]{2,1,0:T(8,128)(2,1)S(1)} %get-tuple-element.4), channel_id=1, source_target_pairs={{1,0},{2,1},{3,2},{4,3},{5,4},{6,5},{7,6},{9,8},{10,9},{11,10},{12... | collective-permute-start | bytes 294920 | tf_op jit(solution)/shard_map/ppermute | solution.py:17
  195.5 0.0 slice-start.1
  195.5 3.3 %collective-permute-start.3 = (bf16[2,32,768]{2,1,0:T(8,128)(2,1)S(1)}, bf16[2,32,768]{2,1,0:T(8,128)(2,1)S(1)}, u32[]{:S(2)}, u32[]{:S(2)}) collective-permute-start(bf16[2,32,768]{2,1,0:T(8,128)(2,1)S(1)} %get-tuple-element.5), channel_id=1, source_target_pairs={{0,1},{1,2},{2,3},{3,4},{4,5},{5,6},{6,7},{8,9},{9,10},{10,11},{11... | collective-permute-start | bytes 294920 | tf_op jit(solution)/shard_map/ppermute | solution.py:14
  198.8 0.0 copy-done.2
  198.8 1.7 fusion.1
  200.5 2.5 %fusion.7 = f32[2,128,1536]{2,1,0:T(8,128)S(1)} fusion(bf16[2,128,768]{2,1,0:T(8,128)(2,1)S(1)} %fusion.29, bf16[3,1536,768]{2,1,0:T(8,128)(2,1)} %all-gather.3.cloned.1.call-done), kind=kOutput, calls=%fused_computation.17 | convolution fusion | flops 603979776 | bytes 4325376 | tf_op jit(solution)/shard_map/wth,ch->wtc/dot_general | solution.py:58
  203.0 0.0 collective-permute-done.3
  203.0 0.0 slice-done
  203.0 0.0 slice-done.1
  203.0 0.8 fusion.9
  203.8 0.0 collective-permute-done.2
  203.9 2.6 %fusion.14 = bf16[2,128,1536]{2,1,0:T(8,128)(2,1)} fusion(bf16[2,128,1536]{2,1,0:T(8,128)(2,1)S(1)} %copy-done, f32[2,128,1536]{2,1,0:T(8,128)S(1)} %fusion.9, f32[2,128,1536]{2,1,0:T(8,128)S(1)} %fusion.7, bf16[3,1536,768]{2,1,0:T(8,128)(2,1)S(1)} %bitcast.31, bf16[2,128,1536]{2,1,0:T(8,128)(2,1)S(1)} %copy-done.3, ...), kind=kOutput, calls=%fused_computation.24 | convolution fusion | flops 614596608 | bytes 8355840 | tf_op jit(solution)/shard_map/wth,ch->wtc/dot_general | solution.py:52
  (6 shorter events, 0.0 us)
Async XLA Ops:
  7.2 1.5 copy-start
  7.2 132.9 %all-gather.3.cloned.1.call-start = ((), (), s32[]{:S(2)}) async-start(), calls=%async_computation | async-start | bytes 8847360 | tf_op jit(solution)/shard_map/all_gather | solution.py:75
  7.9 182.1 %all-gather.5.cloned.1.call-start = ((), (), s32[]{:S(2)}) async-start(), calls=%async_computation.1 | async-start | bytes 2949120 | tf_op jit(solution)/shard_map/all_gather | solution.py:76
  9.2 135.4 %collective-permute-start = (bf16[2,32,1536]{2,1,0:T(8,128)(2,1)S(1)}, bf16[2,32,1536]{2,1,0:T(8,128)(2,1)S(1)}, u32[]{:S(2)}, u32[]{:S(2)}) collective-permute-start(bf16[2,32,1536]{2,1,0:T(8,128)(2,1)S(1)} %get-tuple-element.2), channel_id=1, source_target_pairs={{0,1},{1,2},{2,3},{3,4},{4,5},{5,6},{6,7},{8,9},{9,10},{10,11},{11... | collective-permute-start | bytes 589832 | tf_op jit(solution)/shard_map/ppermute | solution.py:14
  13.8 129.3 %collective-permute-start.1 = (bf16[2,32,1536]{2,1,0:T(8,128)(2,1)S(1)}, bf16[2,32,1536]{2,1,0:T(8,128)(2,1)S(1)}, u32[]{:S(2)}, u32[]{:S(2)}) collective-permute-start(bf16[2,32,1536]{2,1,0:T(8,128)(2,1)S(1)} %get-tuple-element.3), channel_id=1, source_target_pairs={{1,0},{2,1},{3,2},{4,3},{5,4},{6,5},{7,6},{9,8},{10,9},{11,10},{12... | collective-permute-start | bytes 589832 | tf_op jit(solution)/shard_map/ppermute | solution.py:17
  140.1 3.7 %copy-start.1 = (bf16[3,1536,768]{2,1,0:T(8,128)(2,1)S(1)}, bf16[3,1536,768]{2,1,0:T(8,128)(2,1)}, u32[]{:S(2)}) copy-start(bf16[3,1536,768]{2,1,0:T(8,128)(2,1)} %all-gather.3.cloned.1.call-done) | copy-start | bytes 21233668
  144.6 45.4 %copy-start.3 = (bf16[2,128,1536]{2,1,0:T(8,128)(2,1)S(1)}, bf16[2,128,1536]{2,1,0:T(8,128)(2,1)}, u32[]{:S(2)}) copy-start(bf16[2,128,1536]{2,1,0:T(8,128)(2,1)} %param.7) | copy-start | bytes 2359300
  190.0 8.8 %copy-start.2 = (bf16[768,1536]{1,0:T(8,128)(2,1)S(1)}, bf16[768,1536]{1,0:T(8,128)(2,1)}, u32[]{:S(2)}) copy-start(bf16[768,1536]{1,0:T(8,128)(2,1)} %all-gather.5.cloned.1.call-done) | copy-start | bytes 7077892
  190.0 13.0 %slice-start = ((s8[7077888]{0:T(1024)(128)(4,1)}), s8[4194304]{0:T(1024)(128)(4,1)S(1)}, s32[]{:S(2)}) async-start(s8[7077888]{0:T(1024)(128)(4,1)} %bitcast.30), calls=%async_computation.2 | async-start | bytes 8388608
  192.9 11.0 %collective-permute-start.2 = (bf16[2,32,768]{2,1,0:T(8,128)(2,1)S(1)}, bf16[2,32,768]{2,1,0:T(8,128)(2,1)S(1)}, u32[]{:S(2)}, u32[]{:S(2)}) collective-permute-start(bf16[2,32,768]{2,1,0:T(8,128)(2,1)S(1)} %get-tuple-element.4), channel_id=1, source_target_pairs={{1,0},{2,1},{3,2},{4,3},{5,4},{6,5},{7,6},{9,8},{10,9},{11,10},{12... | collective-permute-start | bytes 294920 | tf_op jit(solution)/shard_map/ppermute | solution.py:17
  195.5 7.5 %slice-start.1 = ((s8[7077888]{0:T(1024)(128)(4,1)}), s8[2883584]{0:T(1024)(128)(4,1)S(1)}, s32[]{:S(2)}) async-start(s8[7077888]{0:T(1024)(128)(4,1)} %bitcast.30), calls=%async_computation.3 | async-start | bytes 5767168
  195.5 7.5 %collective-permute-start.3 = (bf16[2,32,768]{2,1,0:T(8,128)(2,1)S(1)}, bf16[2,32,768]{2,1,0:T(8,128)(2,1)S(1)}, u32[]{:S(2)}, u32[]{:S(2)}) collective-permute-start(bf16[2,32,768]{2,1,0:T(8,128)(2,1)S(1)} %get-tuple-element.5), channel_id=1, source_target_pairs={{0,1},{1,2},{2,3},{3,4},{4,5},{5,6},{6,7},{8,9},{9,10},{10,11},{11... | collective-permute-start | bytes 294920 | tf_op jit(solution)/shard_map/ppermute | solution.py:14
Sparse Core Ops, SparseCore 0:
  9.6 130.4 all-gather.2
  141.7 48.2 all-gather.4
where the time goes:
time: 214 us; the launch traced here: 213 us
  waiting for transfers between devices  170 us (79%)
  matrix products  14.9 us (7%)
  between operations  14.2 us (7%)
  starting transfers between devices  12.4 us (6%)
    all_gather x1, waiting for transfers between devices, per_device(): lax.all_gather(dilated_tap_weight, 'dp', axis=1, tiled=True)  124 us
    all_gather x1, waiting for transfers between devices, per_device(): lax.all_gather(out_weight, 'dp', axis=1, tiled=True)  44.6 us
    ppermute x2, starting transfers between devices, extended(): lax.ppermute(lax.slice_in_dim(block, block.shape[dim] - width, None, axis...  7.76 us
    ppermute x2, starting transfers between devices, extended(): lax.ppermute(lax.slice_in_dim(block, 0, width, axis=dim), axis, backward)  4.54 us
  transfers between devices with their start and end apart: 6, of which 2 were waited for; matrix products, arithmetic and copies ran while one was open for 5% of the time, Pallas kernels for 0%

commit v1 on v0

--- a/solution.py
+++ b/solution.py
@@ -2,8 +2,17 @@
 import jax.numpy as jnp
 from jax import lax
 from jax.sharding import PartitionSpec as P
+from jax.lax import axis_index, axis_size, ppermute
 
 DILATION_STEP = 32
+
+
+def rings_list(own_rows, which_dim):
+    own_rows = jnp.moveaxis(own_rows, 0, which_dim)
+    lower = own_rows.shape
+    return own_rows.reshape(
+        *lower[:which_dim], lower[which_dim] * lower[which_dim + 1], *lower[which_dim + 2 :]
+    )
 
 
 def extended(block, sides, width):
@@ -71,9 +80,27 @@
 
 
 def per_device(signal, dilated_tap_weight, out_weight, cotangent):
+
+    def node_derive(x_local, lane_axis, axis_k):
+        axis_n = axis_size(lane_axis)
+        buffers = [(at, (at + 1) % axis_n) for at in range(axis_n)]
+        by_place = [(j, ii) for ii, j in buffers]
+        value_now, even = ([], [])
+        for no in range(axis_n - 1):
+            if no % 2 == 0:
+                value_now.append(
+                    ppermute(value_now[-1] if value_now else x_local, lane_axis, buffers)
+                )
+            else:
+                even.append(ppermute(even[-1] if even else x_local, lane_axis, by_place))
+        ready = jnp.stack([*value_now[::-1], x_local, *even])
+        f_next = axis_index(lane_axis) - len(value_now)
+        ready = ready[(jnp.arange(axis_n) - f_next) % axis_n]
+        return rings_list(ready, axis_k)
+
     convolution_filter, output_map = (
         lax.all_gather(dilated_tap_weight, "dp", axis=1, tiled=True),
-        lax.all_gather(out_weight, "dp", axis=1, tiled=True),
+        node_derive(out_weight, "dp", 1),
     )
     signal_wide = signal.astype(jnp.float32)
     gelu_output = jax.nn.gelu(signal_wide).astype(jnp.bfloat16)

time: 214 us -> 196 us (0.916)
  waiting for transfers between devices: 170 us -> 128 us
  starting transfers between devices: 12.4 us -> 27.8 us
  local copies, waits for them, and re-layouts: 0.86 us -> 7.9 us
    all_gather x1 -> x0, waiting for transfers between devices: 44.6 us -> none  [per_device(): lax.all_gather(out_weight, 'dp', axis=1, tiled=True)]
    ppermute x0 -> x3, waiting for transfers between devices: none -> 44 us  [the longest x1 23.3 us: node_derive(): even.append(ppermute(even[-1] if even else x_local, lane_axis, by_place))]
    all_gather x1, waiting for transfers between devices: 124 us -> 82.2 us  [per_device(): lax.all_gather(dilated_tap_weight, 'dp', axis=1, tiled=True)]
    ppermute x2, starting transfers between devices: 7.76 us -> 19.3 us  [extended(): lax.ppermute(lax.slice_in_dim(block, block.shape[dim] - width, None, axis...]
    ppermute x0 -> x3, starting transfers between devices: none -> 4.16 us  [the longest x2 2.13 us: node_derive(): ppermute(value_now[-1] if value_now else x_local, lane_axis, buffers)]
    transpose x0 -> x1, local copies, waits for them, and re-layouts: none -> 2.85 us  [rings_list(): own_rows = jnp.moveaxis(own_rows, 0, which_dim)]
    gather x0 -> x1, local copies, waits for them, and re-layouts: none -> 2.36 us  [node_derive(): ready = ready[(jnp.arange(axis_n) - f_next) % axis_n]]
  transfers between devices with their start and end apart: 6 -> 8, of which waited for: 2 -> 5; matrix products, arithmetic and copies ran while one was open for 5% -> 8% of each run, Pallas kernels for 0% -> 0%
where the time goes in v1:
time: 196 us; the launch traced here: 194 us
  waiting for transfers between devices  128 us (65%)
  starting transfers between devices  27.8 us (14%)
  between operations  14.2 us (7%)
  matrix products  13.8 us (7%)
  local copies, waits for them, and re-layouts  7.9 us (4%)
  other arithmetic  2.53 us (1%)
    all_gather x1, waiting for transfers between devices, per_device(): lax.all_gather(dilated_tap_weight, 'dp', axis=1, tiled=True)  82.2 us
    ppermute x1, waiting for transfers between devices, node_derive(): even.append(ppermute(even[-1] if even else x_local, lane_axis, by_place))  23.3 us
    ppermute x2, waiting for transfers between devices, node_derive(): ppermute(value_now[-1] if value_now else x_local, lane_axis, buffers)  20.7 us
    ppermute x2, starting transfers between devices, extended(): lax.ppermute(lax.slice_in_dim(block, block.shape[dim] - width, None, axis...  19.3 us
    ppermute x2, starting transfers between devices, extended(): lax.ppermute(lax.slice_in_dim(block, 0, width, axis=dim), axis, backward)  4.28 us
  transfers between devices with their start and end apart: 8, of which 5 were waited for; matrix products, arithmetic and copies ran while one was open for 8% of the time, Pallas kernels for 0%

profile of v1, /device:TPU:1, one launch (start us, length us, event | category | flops | bytes accessed | tf_op | source)
XLA Modules:
  0.0 193.9 jit_solution(14885305589910751036)
XLA Ops:
  7.2 0.0 copy-start.2
  7.2 0.0 copy-start
  7.2 0.0 all-gather.2.cloned.1.call-start
  7.2 0.7 all-gather.2.cloned.1.call-update
  7.9 0.3 copy-done.2
  8.2 2.1 %collective-permute-start.2 = (bf16[768,384]{1,0:T(8,128)(2,1)S(1)}, bf16[768,384]{1,0:T(8,128)(2,1)S(1)}, u32[]{:S(2)}, u32[]{:S(2)}) collective-permute-start(bf16[768,384]{1,0:T(8,128)(2,1)S(1)} %copy-done.2), channel_id=1, source_target_pairs={{0,8},{8,16},{16,24},{24,0},{1,9},{9,17},{17,25},{25,1},{2,10},{10... | collective-permute-start | bytes 1769480 | tf_op jit(solution)/shard_map/ppermute | solution.py:92
  10.4 2.0 %collective-permute-start.4 = (bf16[768,384]{1,0:T(8,128)(2,1)S(1)}, bf16[768,384]{1,0:T(8,128)(2,1)S(1)}, u32[]{:S(2)}, u32[]{:S(2)}) collective-permute-start(bf16[768,384]{1,0:T(8,128)(2,1)S(1)} %copy-done.2), channel_id=1, source_target_pairs={{8,0},{16,8},{24,16},{0,24},{9,1},{17,9},{25,17},{1,25},{10,2},{18... | collective-permute-start | bytes 1769480 | tf_op jit(solution)/shard_map/ppermute | solution.py:95
  12.4 0.5 fusion.15
  12.9 12.5 %collective-permute-done.2 = bf16[768,384]{1,0:T(8,128)(2,1)S(1)} collective-permute-done((bf16[768,384]{1,0:T(8,128)(2,1)S(1)}, bf16[768,384]{1,0:T(8,128)(2,1)S(1)}, u32[]{:S(2)}, u32[]{:S(2)}) %collective-permute-start.2) | collective-permute-done | bytes 589856 | tf_op jit(solution)/shard_map/ppermute | solution.py:92
  25.5 0.8 fusion.46
  26.2 16.1 %collective-permute-start = (bf16[2,32,1536]{2,1,0:T(8,128)(2,1)S(1)}, bf16[2,32,1536]{2,1,0:T(8,128)(2,1)}, u32[]{:S(2)}, u32[]{:S(2)}) collective-permute-start(bf16[2,32,1536]{2,1,0:T(8,128)(2,1)S(1)} %get-tuple-element.2), channel_id=1, source_target_pairs={{0,1},{1,2},{2,3},{3,4},{4,5},{5,6},{6,7},{8,9},{9,10},{10,11},{11... | collective-permute-start | bytes 589832 | tf_op jit(solution)/shard_map/ppermute | solution.py:23
  42.3 1.9 collective-permute-start.1
  44.3 23.3 %collective-permute-done.4 = bf16[768,384]{1,0:T(8,128)(2,1)S(1)} collective-permute-done((bf16[768,384]{1,0:T(8,128)(2,1)S(1)}, bf16[768,384]{1,0:T(8,128)(2,1)S(1)}, u32[]{:S(2)}, u32[]{:S(2)}) %collective-permute-start.4) | collective-permute-done | bytes 589856 | tf_op jit(solution)/shard_map/ppermute | solution.py:95
  67.6 8.2 %collective-permute-done.3 = bf16[768,384]{1,0:T(8,128)(2,1)S(1)} collective-permute-done((bf16[768,384]{1,0:T(8,128)(2,1)S(1)}, bf16[768,384]{1,0:T(8,128)(2,1)S(1)}, u32[]{:S(2)}, u32[]{:S(2)}) %collective-permute-start.3) | collective-permute-done | bytes 589856 | tf_op jit(solution)/shard_map/ppermute | solution.py:92
  75.8 0.8 copy-done.5
  76.6 2.0 %pad_maximum_fusion = bf16[4,768,384]{2,1,0:T(8,128)(2,1)S(1)} fusion(bf16[1,768,384]{2,1,0:T(8,128)(2,1)} %bitcast.45, bf16[1,768,384]{2,1,0:T(8,128)(2,1)} %bitcast.43, bf16[1,768,384]{2,1,0:T(8,128)(2,1)} %bitcast.44, bf16[1,768,384]{2,1,0:T(8,128)(2,1)} %bitcast.46), kind=kLoop, calls=%fused_computation.13 | loop fusion | flops 3538944 | bytes 4718592 | tf_op jit(solution)/shard_map/stack | solution.py:96
  78.5 2.4 %gather_fusion = bf16[4,768,384]{2,1,0:T(8,128)(2,1)} fusion(bf16[4,768,384]{2,1,0:T(8,128)(2,1)S(1)} %pad_maximum_fusion, s32[1024]{0:T(1024)S(1)} %pad_clamp_fusion), kind=kCustom, calls=%fused_computation | custom fusion | bytes 4718608 | tf_op jit(solution)/shard_map/gather | solution.py:98
  80.9 2.8 %copy.8 = bf16[768,4,384]{0,2,1:T(8,128)(2,1)S(1)} copy(bf16[768,4,384]{2,0,1:T(8,128)(2,1)} %bitcast.40) | data formatting | bytes 4718592 | tf_op jit(solution)/shard_map/transpose | solution.py:11
  83.8 82.2 %all-gather.2.cloned.1.call-done = bf16[3,1536,768]{2,1,0:T(8,128)(2,1)} async-done(((bf16[3,384,768]{2,1,0:T(8,128)(2,1)}), bf16[3,1536,768]{2,1,0:T(8,128)(2,1)}) %all-gather.2.cloned.1.call-update) | async-done | bytes 7077904 | tf_op jit(solution)/shard_map/all_gather | solution.py:102
  165.9 3.1 %fusion.5 = f32[2,128,768]{2,1,0:T(8,128)S(1)} fusion(bf16[3,1536,768]{2,1,0:T(8,128)(2,1)} %all-gather.2.cloned.1.call-done, bf16[2,128,1536]{2,1,0:T(8,128)(2,1)} %param.4), kind=kOutput, calls=%fused_computation.17 | convolution fusion | flops 607911936 | bytes 3932160 | tf_op jit(solution)/shard_map/xzi,iv->xzv/dot_general | solution.py:44
  169.1 0.8 copy-done.6
  169.9 1.7 fusion.7
  171.6 1.8 fusion.19
  173.4 0.0 copy-start.7
  173.4 1.8 fusion.1
  175.2 1.2 fusion.26
  176.4 2.4 %collective-permute-start.5 = (bf16[2,32,768]{2,1,0:T(8,128)(2,1)S(1)}, bf16[2,32,768]{2,1,0:T(8,128)(2,1)S(1)}, u32[]{:S(2)}, u32[]{:S(2)}) collective-permute-start(bf16[2,32,768]{2,1,0:T(8,128)(2,1)S(1)} %get-tuple-element.4), channel_id=1, source_target_pairs={{1,0},{2,1},{3,2},{4,3},{5,4},{6,5},{7,6},{9,8},{10,9},{11,10},{12... | collective-permute-start | bytes 294920 | tf_op jit(solution)/shard_map/ppermute | solution.py:26
  178.8 3.2 %collective-permute-start.6 = (bf16[2,32,768]{2,1,0:T(8,128)(2,1)S(1)}, bf16[2,32,768]{2,1,0:T(8,128)(2,1)S(1)}, u32[]{:S(2)}, u32[]{:S(2)}) collective-permute-start(bf16[2,32,768]{2,1,0:T(8,128)(2,1)S(1)} %get-tuple-element.5), channel_id=1, source_target_pairs={{0,1},{1,2},{2,3},{3,4},{4,5},{5,6},{6,7},{8,9},{9,10},{10,11},{11... | collective-permute-start | bytes 294920 | tf_op jit(solution)/shard_map/ppermute | solution.py:23
  182.0 0.8 fusion.4
  182.8 0.8 collective-permute-done.6
  183.6 0.8 fusion.6
  184.4 2.6 %fusion.11 = bf16[2,128,1536]{2,1,0:T(8,128)(2,1)} fusion(bf16[2,128,1536]{2,1,0:T(8,128)(2,1)S(1)} %copy-done.1, f32[2,128,1536]{2,1,0:T(8,128)S(1)} %fusion.6, f32[2,128,1536]{2,1,0:T(8,128)S(1)} %fusion.4, bf16[3,1536,768]{2,1,0:T(8,128)(2,1)S(1)} %copy-done.6, bf16[2,128,1536]{2,1,0:T(8,128)(2,1)S(1)} %copy-done.7, ...), kind=kOutput, calls=%fused_computation.23 | convolution fusion | flops 614596608 | bytes 8355840 | tf_op jit(solution)/shard_map/wth,ch->wtc/dot_general | solution.py:61
  (17 shorter events, 0.1 us)
Async XLA Ops:
  7.2 1.1 copy-start.2
  7.2 5.2 %copy-start = (bf16[2,128,1536]{2,1,0:T(8,128)(2,1)S(1)}, bf16[2,128,1536]{2,1,0:T(8,128)(2,1)}, u32[]{:S(2)}) copy-start(bf16[2,128,1536]{2,1,0:T(8,128)(2,1)} %param.4) | copy-start | bytes 2359300
  7.2 158.8 %all-gather.2.cloned.1.call-start = ((), (), s32[]{:S(2)}) async-start(), calls=%async_computation | async-start | bytes 8847360 | tf_op jit(solution)/shard_map/all_gather | solution.py:102
  8.2 17.2 %collective-permute-start.2 = (bf16[768,384]{1,0:T(8,128)(2,1)S(1)}, bf16[768,384]{1,0:T(8,128)(2,1)S(1)}, u32[]{:S(2)}, u32[]{:S(2)}) collective-permute-start(bf16[768,384]{1,0:T(8,128)(2,1)S(1)} %copy-done.2), channel_id=1, source_target_pairs={{0,8},{8,16},{16,24},{24,0},{1,9},{9,17},{17,25},{25,1},{2,10},{10... | collective-permute-start | bytes 1769480 | tf_op jit(solution)/shard_map/ppermute | solution.py:92
  10.4 57.2 %collective-permute-start.4 = (bf16[768,384]{1,0:T(8,128)(2,1)S(1)}, bf16[768,384]{1,0:T(8,128)(2,1)S(1)}, u32[]{:S(2)}, u32[]{:S(2)}) collective-permute-start(bf16[768,384]{1,0:T(8,128)(2,1)S(1)} %copy-done.2), channel_id=1, source_target_pairs={{8,0},{16,8},{24,16},{0,24},{9,1},{17,9},{25,17},{1,25},{10,2},{18... | collective-permute-start | bytes 1769480 | tf_op jit(solution)/shard_map/ppermute | solution.py:95
  25.5 50.3 %copy-start.3 = (bf16[768,384]{1,0:T(8,128)(2,1)}, bf16[768,384]{1,0:T(8,128)(2,1)S(1)}, u32[]{:S(2)}) copy-start(bf16[768,384]{1,0:T(8,128)(2,1)S(1)} %collective-permute-done.2) | copy-start | bytes 1769476
  25.5 50.3 %collective-permute-start.3 = (bf16[768,384]{1,0:T(8,128)(2,1)S(1)}, bf16[768,384]{1,0:T(8,128)(2,1)S(1)}, u32[]{:S(2)}, u32[]{:S(2)}) collective-permute-start(bf16[768,384]{1,0:T(8,128)(2,1)S(1)} %collective-permute-done.2), channel_id=1, source_target_pairs={{0,8},{8,16},{16,24},{24,0},{1,9},{9,17},{17,25},{25,1},{2,10},{10... | collective-permute-start | bytes 1769480 | tf_op jit(solution)/shard_map/ppermute | solution.py:92
  26.2 145.4 %collective-permute-start = (bf16[2,32,1536]{2,1,0:T(8,128)(2,1)S(1)}, bf16[2,32,1536]{2,1,0:T(8,128)(2,1)}, u32[]{:S(2)}, u32[]{:S(2)}) collective-permute-start(bf16[2,32,1536]{2,1,0:T(8,128)(2,1)S(1)} %get-tuple-element.2), channel_id=1, source_target_pairs={{0,1},{1,2},{2,3},{3,4},{4,5},{5,6},{6,7},{8,9},{9,10},{10,11},{11... | collective-permute-start | bytes 589832 | tf_op jit(solution)/shard_map/ppermute | solution.py:23
  42.3 126.8 %collective-permute-start.1 = (bf16[2,32,1536]{2,1,0:T(8,128)(2,1)}, bf16[2,32,1536]{2,1,0:T(8,128)(2,1)}, u32[]{:S(2)}, u32[]{:S(2)}) collective-permute-start(bf16[2,32,1536]{2,1,0:T(8,128)(2,1)} %get-tuple-element.3), channel_id=1, source_target_pairs={{1,0},{2,1},{3,2},{4,3},{5,4},{6,5},{7,6},{9,8},{10,9},{11,10},{12... | collective-permute-start | bytes 589832 | tf_op jit(solution)/shard_map/ppermute | solution.py:26
  67.6 8.2 %copy-start.4 = (bf16[768,384]{1,0:T(8,128)(2,1)}, bf16[768,384]{1,0:T(8,128)(2,1)S(1)}, u32[]{:S(2)}) copy-start(bf16[768,384]{1,0:T(8,128)(2,1)S(1)} %collective-permute-done.4) | copy-start | bytes 1769476
  75.8 0.8 copy-start.5
  165.9 4.0 %copy-start.6 = (bf16[3,1536,768]{2,1,0:T(8,128)(2,1)S(1)}, bf16[3,1536,768]{2,1,0:T(8,128)(2,1)}, u32[]{:S(2)}) copy-start(bf16[3,1536,768]{2,1,0:T(8,128)(2,1)} %all-gather.2.cloned.1.call-done) | copy-start | bytes 21233668
  171.6 1.8 copy-start.1
  173.4 1.8 copy-start.7
  176.4 8.0 %collective-permute-start.5 = (bf16[2,32,768]{2,1,0:T(8,128)(2,1)S(1)}, bf16[2,32,768]{2,1,0:T(8,128)(2,1)S(1)}, u32[]{:S(2)}, u32[]{:S(2)}) collective-permute-start(bf16[2,32,768]{2,1,0:T(8,128)(2,1)S(1)} %get-tuple-element.4), channel_id=1, source_target_pairs={{1,0},{2,1},{3,2},{4,3},{5,4},{6,5},{7,6},{9,8},{10,9},{11,10},{12... | collective-permute-start | bytes 294920 | tf_op jit(solution)/shard_map/ppermute | solution.py:26
  178.8 4.8 %collective-permute-start.6 = (bf16[2,32,768]{2,1,0:T(8,128)(2,1)S(1)}, bf16[2,32,768]{2,1,0:T(8,128)(2,1)S(1)}, u32[]{:S(2)}, u32[]{:S(2)}) collective-permute-start(bf16[2,32,768]{2,1,0:T(8,128)(2,1)S(1)} %get-tuple-element.5), channel_id=1, source_target_pairs={{0,1},{1,2},{2,3},{3,4},{4,5},{5,6},{6,7},{8,9},{9,10},{10,11},{11... | collective-permute-start | bytes 294920 | tf_op jit(solution)/shard_map/ppermute | solution.py:23
Sparse Core Ops, SparseCore 0:
  9.6 156.3 all-gather.1
